TPU v7x, 128 devices: a whole 4x4x4 slice. The times are simulated.
128 devices in a mesh: req: 8 (over y, core), tok: 16 (over x, z).
Axes of the slice: x: 4, y: 4, z: 4, core: 2. Of those that a mesh axis runs over, the one named last changes fastest.
Arguments:
- layer_input: bfloat16 [16384, 2048], P(('req', 'tok')), may hold values from -12 to 12
- q_in: bfloat16 [16384, 2048], P(('req', 'tok')), may hold values from -10 to 10
- k_in: bfloat16 [16384, 2048], P(('req', 'tok')), may hold values from -10 to 10
- v_in: bfloat16 [16384, 2048], P(('req', 'tok')), may hold values from -6 to 6
- segment_ids: int32 [8, 2048], P('req'), may hold values from 0 to 3, never falling along the last dimension, each value on 1 to 1024 neighbouring positions
- lambda_parts: float32 [4, 128], replicated, may hold values from -0.8 to 0.8
- out_weight: bfloat16 [2048, 2048], replicated, may hold values from -0.125 to 0.125
- ffn_gain: float32 [2048], replicated, may hold values from 0.1 to 1.9
- gate_weight: bfloat16 [2048, 5632], P(None, 'req'), may hold values from -0.125 to 0.125
- up_weight: bfloat16 [2048, 5632], P(None, 'req'), may hold values from -0.125 to 0.125
- down_weight: bfloat16 [5632, 2048], P('req'), may hold values from -0.078125 to 0.078125
- next_gain: float32 [2048], replicated, may hold values from 0.1 to 1.9
- qkv_weight: bfloat16 [2048, 6144], P(None, 'req'), may hold values from -0.125 to 0.125
- page_owner: int32 [8, 256], P('req'), may hold values from 0 to 15, as said below
- page_slot: int32 [8, 256], P('req'), may hold values from 0 to 15, as said below
Outputs:
- layer_output: bfloat16 [16384, 2048], P(('req', 'tok'))
- q_next: bfloat16 [16384, 2048], P(('req', 'tok'))
- page_cache: bfloat16 [2048, 8, 4096], P(('req', 'tok'))
Inputs may be any that keep to these rules, and one draw needn't show every extreme that they name: `segment_ids`: segment numbers never fall along a group; each of the 4 prompts of a group has 1 to 1024 tokens, one exactly 1024. `page_owner`: the 16 pages of each device name every device of its request group as owner exactly once. `page_slot`: within a request group every pair of owner and slot is named by exactly one page.
All inputs are finite; a program needn't handle non-finite values.
Results may differ from a plain program's by a relative error of at most 0.017.
Values may be sent and summed in bfloat16 or wider, within the bound.
A program may use at most 192 MiB of HBM per device.

v0:
```python
import math
import jax
import jax.numpy as jnp
from jax import lax
from jax.sharding import PartitionSpec as P

HEADS = 8
PAGE = 8
NEG_FILL = -1e30
LAMBDA_INIT = 0.2
EPSILON = 1e-05
MAX_SEG = 1024


def rms_rows(values):
    return values * lax.rsqrt(jnp.mean(values * values, axis=-1, keepdims=True) + EPSILON)


def lambda_value(lambda_parts):
    first_term = jnp.exp(jnp.sum(lambda_parts[0] * lambda_parts[1]))
    second_term = jnp.exp(jnp.sum(lambda_parts[2] * lambda_parts[3]))
    return first_term - second_term + LAMBDA_INIT


def body(
    layer_input,
    q_in,
    k_in,
    v_in,
    segment_ids,
    lambda_parts,
    out_weight,
    ffn_gain,
    gate_weight,
    up_weight,
    down_weight,
    next_gain,
    qkv_weight,
    page_owner,
    page_slot,
):
    row_count = q_in.shape[0]
    feat_width = q_in.shape[1]
    head_dim = feat_width // (2 * HEADS)
    peer_count = lax.axis_size("tok")
    tok_place = lax.axis_index("tok")
    seg_row = segment_ids[0]
    first_row = tok_place * row_count
    query_places = first_row + jnp.arange(row_count)
    query_segs = lax.dynamic_slice_in_dim(seg_row, first_row, row_count)
    lambda_mix = lambda_value(lambda_parts)
    score_scale = 1.0 / math.sqrt(head_dim)
    query_split = q_in.reshape(row_count, HEADS, 2, head_dim)
    run_max = jnp.full((HEADS, 2, row_count), NEG_FILL, jnp.float32)
    back = -(-(MAX_SEG - 1) // row_count)
    own_kv = jnp.concatenate([k_in, v_in], axis=1)
    all_kv = lax.all_gather(own_kv, "tok", axis=0, tiled=True)
    padded_kv = jnp.concatenate(
        [jnp.zeros((back * row_count, 2 * feat_width), all_kv.dtype), all_kv], axis=0
    )
    window = lax.dynamic_slice_in_dim(padded_kv, first_row, (back + 1) * row_count, 0)
    piece_len = window.shape[0]
    key_rows = window[:, :feat_width]
    value_rows = window[:, feat_width:]
    key_split = key_rows.reshape(piece_len, HEADS, 2, head_dim)
    value_split = value_rows.reshape(piece_len, HEADS, 2 * head_dim)
    key_places = (tok_place - back) * row_count + jnp.arange(piece_len)
    key_segs = jnp.take(seg_row, jnp.clip(key_places, 0, seg_row.shape[0] - 1))
    visible = (
        (key_places[None, :] >= 0)
        & (key_segs[None, :] == query_segs[:, None])
        & (key_places[None, :] <= query_places[:, None])
    )
    scores = (
        jnp.einsum("qhmd,khmd->hmqk", query_split, key_split, preferred_element_type=jnp.float32)
        * score_scale
    )
    scores = jnp.where(visible, scores, NEG_FILL)
    new_max = jnp.maximum(run_max, jnp.max(scores, axis=-1))
    weights = jnp.where(visible, jnp.exp(scores - new_max[..., None]), 0.0)
    totals = jnp.sum(weights, axis=-1)
    weighted = jnp.einsum(
        "hmqk,khe->hmqe",
        weights.astype(jnp.bfloat16),
        value_split,
        preferred_element_type=jnp.float32,
    )
    run_max, totals, weighted = (new_max, totals, weighted)
    map_outputs = weighted / totals[..., None]
    difference = map_outputs[:, 0] - lambda_mix * map_outputs[:, 1]
    head_outputs = rms_rows(difference) * (1.0 - LAMBDA_INIT)
    attention = (
        jnp.transpose(head_outputs, (1, 0, 2)).reshape(row_count, feat_width).astype(jnp.bfloat16)
    )
    residual_mid = (
        layer_input.astype(jnp.float32)
        + jnp.dot(attention, out_weight, preferred_element_type=jnp.float32)
    ).astype(jnp.bfloat16)
    gathered = lax.all_gather(residual_mid, "req", axis=0, tiled=True)
    normed = (rms_rows(gathered.astype(jnp.float32)) * ffn_gain).astype(jnp.bfloat16)
    gate_proj = jnp.dot(normed, gate_weight, preferred_element_type=jnp.float32)
    up_proj = jnp.dot(normed, up_weight, preferred_element_type=jnp.float32)
    hidden = (jax.nn.silu(gate_proj) * up_proj).astype(jnp.bfloat16)
    ffn_own = lax.psum_scatter(
        jnp.dot(hidden, down_weight, preferred_element_type=jnp.float32).astype(jnp.bfloat16),
        "req",
        scatter_dimension=0,
        tiled=True,
    ).astype(jnp.float32)
    layer_output = (residual_mid.astype(jnp.float32) + ffn_own).astype(jnp.bfloat16)
    next_normed = (rms_rows(layer_output.astype(jnp.float32)) * next_gain).astype(jnp.bfloat16)
    projected_cols = jnp.dot(
        lax.all_gather(next_normed, "req", axis=0, tiled=True),
        qkv_weight,
        preferred_element_type=jnp.float32,
    ).astype(jnp.bfloat16)
    projected = lax.all_to_all(projected_cols, "req", split_axis=0, concat_axis=1, tiled=True)
    q_next = projected[:, :feat_width]
    pages_dev = row_count // PAGE
    per_owner = pages_dev // peer_count
    key_values = projected[:, feat_width:].reshape(pages_dev, PAGE, 2 * feat_width)
    owner_all = page_owner[0].reshape(peer_count, pages_dev)
    slot_all = page_slot[0].reshape(peer_count, pages_dev)
    page_numbers = jnp.arange(pages_dev, dtype=jnp.int32)
    my_owners = lax.dynamic_index_in_dim(owner_all, tok_place, 0, keepdims=False)
    send_order = jnp.argsort(my_owners * pages_dev + page_numbers)
    outgoing = key_values[send_order].reshape(peer_count, per_owner, PAGE, 2 * feat_width)
    incoming = lax.all_to_all(outgoing, "tok", split_axis=0, concat_axis=0, tiled=True)
    rank_keys = jnp.where(
        owner_all == tok_place, page_numbers[None, :], pages_dev + page_numbers[None, :]
    )
    chosen_pages = jnp.argsort(rank_keys, axis=1)[:, :per_owner]
    slot_list = jnp.take_along_axis(slot_all, chosen_pages, axis=1).reshape(pages_dev)
    page_cache = (
        jnp.zeros((pages_dev, PAGE, 2 * feat_width), jnp.bfloat16)
        .at[slot_list]
        .set(incoming.reshape(pages_dev, PAGE, 2 * feat_width))
    )
    return (layer_output, q_next, page_cache)


def solution(mesh):
    in_specs = (
        P(("req", "tok"), None),
        P(("req", "tok"), None),
        P(("req", "tok"), None),
        P(("req", "tok"), None),
        P("req", None),
        P(),
        P(),
        P(),
        P(None, "req"),
        P(None, "req"),
        P("req", None),
        P(),
        P(None, "req"),
        P("req", None),
        P("req", None),
    )
    out_specs = (P(("req", "tok"), None), P(("req", "tok"), None), P(("req", "tok"), None, None))
    return jax.shard_map(body, mesh=mesh, in_specs=in_specs, out_specs=out_specs, check_vma=False)
```

profile of v0, /device:TPU:0, one launch (start us, length us, event | category | flops | bytes accessed | tf_op | source)
XLA Modules:
  0.0 369.7 jit_solution(3113207393178205079)
XLA Ops:
  7.2 2.2 copy.38
  9.4 2.0 copy.39
  11.5 2.2 pad_maximum_fusion
  13.8 2.2 reshape.141
  18.0 6.5 %gather_fusion = s32[1152]{0:T(1024)S(1)} fusion(s32[2048]{0:T(1024)S(1)} %bitcast.64, s32[2048]{0:T(1024)S(1)} %pad_clamp_fusion), kind=kCustom, calls=%fused_computation | custom fusion | bytes 13824 | tf_op jit(solution)/shard_map/jit(_take)/gather | solution.py:68
  25.6 112.0 %all-gather.4.cloned.1.call-done = bf16[2048,4096]{0,1:T(8,128)(2,1)} async-done(((bf16[128,4096]{0,1:T(8,128)(2,1)}), bf16[2048,4096]{0,1:T(8,128)(2,1)}) %all-gather.4.cloned.1.call-update) | async-done | bytes 16777232 | tf_op jit(solution)/shard_map/all_gather | solution.py:57
  137.5 5.1 %pad_dynamic-slice_fusion.1 = (bf16[1152,2048]{0,1:T(8,128)(2,1)}, bf16[1152,2048]{0,1:T(8,128)(2,1)S(1)}) fusion(s32[]{:T(128)S(6)} %select_n.70, s32[]{:T(128)S(6)} %add.181, bf16[2048,4096]{0,1:T(8,128)(2,1)} %all-gather.4.cloned.1.call-done), kind=kLoop, calls=%fused_computation.5 | loop fusion | bytes 26214408 | tf_op jit(solution)/shard_map/slice | solution.py:64
  142.6 2.5 fusion.3
  145.1 2.3 fusion.4
  147.4 1.3 copy-done.2
  148.7 8.3 %broadcast_divide_fusion = f32[8,2,128,256]{3,2,1,0:T(8,128)S(1)} fusion(f32[8,2,128]{2,1,0:T(2,128)S(1)} %fusion.4, bf16[1152,8,256,1]{0,2,3,1:T(8,128)(2,1)} %bitcast.68, f32[8,2,1152,128]{3,2,1,0:T(8,128)} %copy-done.2, f32[8,2,128]{2,1,0:T(2,128)S(1)} %broadcast_maximum_fusion, pred[128,1152]{0,1:T(8,128)(4,1)S(1)} %compare_and_fusion), kind=kOutput, calls=%fused_computation.41 | convolution fusion | flops 1220280320 | bytes 16416768 | tf_op jit(solution)/shard_map/hmqk,khe->hmqe/dot_general | solution.py:82
  157.2 1.1 fusion.26
  158.3 2.0 copy.44
  160.3 5.7 %fusion.13 = bf16[128,2048]{1,0:T(8,128)(2,1)} fusion(bf16[128,2048]{0,1:T(8,128)(2,1)} %bitcast.70, bf16[2048,2048]{1,0:T(8,128)(2,1)} %param.21, bf16[128,2048]{1,0:T(8,128)(2,1)} %param.15), kind=kOutput, calls=%fused_computation.25 | convolution fusion | flops 1074528256 | bytes 9961472 | tf_op jit(solution)/shard_map/dot_general | solution.py:97
  166.3 33.9 %all-gather.6.cloned.1.call-done = bf16[1024,2048]{1,0:T(8,128)(2,1)} async-done(((bf16[128,2048]{1,0:T(8,128)(2,1)}), bf16[1024,2048]{1,0:T(8,128)(2,1)}) %all-gather.6.cloned.1.call-update) | async-done | bytes 4194320 | tf_op jit(solution)/shard_map/all_gather | solution.py:99
  200.1 3.2 fusion
  203.6 6.7 %fusion.15 = f32[1024,704]{0,1:T(8,128)} fusion(bf16[2048,704]{0,1:T(8,128)(2,1)} %param.23, bf16[1024,2048]{1,0:T(8,128)(2,1)S(1)} %copy-done.4, f32[2048]{0:T(1024)S(1)} %copy-done.11, f32[1024]{0:T(1024)S(1)} %add_rsqrt_fusion), kind=kOutput, calls=%fused_computation.29 | convolution fusion | flops 2961178624 | bytes 9973760 | tf_op jit(solution)/shard_map/dot_general | solution.py:101
  210.3 12.4 %convolution_convert_fusion = bf16[1024,2048]{1,0:T(8,128)(2,1)} fusion(bf16[704,2048]{1,0:T(8,128)(2,1)} %param.25, f32[1024,704]{0,1:T(8,128)} %fusion.15, bf16[2048,704]{0,1:T(8,128)(2,1)} %param.24, bf16[1024,2048]{1,0:T(8,128)(2,1)} %all-gather.6.cloned.1.call-done, f32[2048]{0:T(1024)S(1)} %copy-done.11, f32[1024]{0:T(1024)S(1)} %add_rsqrt_fusion), kind=kOutput, calls=%fused_computation.22 | convolution fusion | flops 5920391168 | bytes 17051648 | tf_op jit(solution)/shard_map/dot_general | solution.py:105
  222.8 37.9 %reduce-scatter.2.cloned.1.call-done = bf16[128,2048]{1,0:T(8,128)(2,1)} async-done(((bf16[1024,2048]{1,0:T(8,128)(2,1)}), bf16[128,2048]{1,0:T(8,128)(2,1)}) %reduce-scatter.2.cloned.1.call-update) | async-done | bytes 524304 | tf_op jit(solution)/shard_map/reduce_scatter | solution.py:104
  260.6 1.5 fusion.19
  263.9 31.2 %all-gather.8.cloned.1.call-done = bf16[1024,2048]{1,0:T(8,128)(2,1)} async-done(((bf16[128,2048]{1,0:T(8,128)(2,1)}), bf16[1024,2048]{1,0:T(8,128)(2,1)}) %all-gather.8.cloned.1.call-update) | async-done | bytes 4194320 | tf_op jit(solution)/shard_map/all_gather | solution.py:113
  295.1 6.8 %convolution_convert_fusion.1 = bf16[1024,768]{1,0:T(8,128)(2,1)} fusion(bf16[1024,2048]{1,0:T(8,128)(2,1)} %all-gather.8.cloned.1.call-done, bf16[2048,768]{1,0:T(8,128)(2,1)S(1)} %copy-done), kind=kOutput, calls=%fused_computation.26 | convolution fusion | flops 3222011904 | bytes 8912896 | tf_op jit(solution)/shard_map/dot_general | solution.py:112
  301.8 4.3 %all-to-all-start = ((bf16[8,128,768]{2,1,0:T(8,128)(2,1)}), bf16[8,128,768]{2,1,0:T(8,128)(2,1)}, u32[]{:S(2)}, u32[]{:S(2)}) async-start(bf16[8,128,768]{2,1,0:T(8,128)(2,1)} %bitcast.71), calls=%async_computation.1 | async-start | bytes 3145728 | tf_op jit(solution)/shard_map/all_to_all | solution.py:117
  308.2 1.2 sort.35
  309.5 18.2 %all-to-all-done = bf16[8,128,768]{2,1,0:T(8,128)(2,1)} async-done(((bf16[8,128,768]{2,1,0:T(8,128)(2,1)}), bf16[8,128,768]{2,1,0:T(8,128)(2,1)}, u32[]{:S(2)}, u32[]{:S(2)}) %all-to-all-start) | async-done | bytes 1572896 | tf_op jit(solution)/shard_map/all_to_all | solution.py:117
  327.7 1.6 copy.52
  329.3 1.1 copy-done.3
  331.5 2.8 gather_fusion.1
  334.3 7.0 %all-to-all-start.1 = ((bf16[16,1,8,4096]{3,2,1,0:T(8,128)(2,1)}), bf16[16,1,8,4096]{3,2,1,0:T(8,128)(2,1)}, u32[]{:S(2)}, u32[]{:S(2)}) async-start(bf16[16,1,8,4096]{3,2,1,0:T(8,128)(2,1)} %bitcast.69), calls=%async_computation.2 | async-start | bytes 2097152 | tf_op jit(solution)/shard_map/all_to_all | solution.py:128
  342.8 1.9 slice.52
  344.7 14.1 %all-to-all-done.1 = bf16[16,1,8,4096]{3,2,1,0:T(8,128)(2,1)} async-done(((bf16[16,1,8,4096]{3,2,1,0:T(8,128)(2,1)}), bf16[16,1,8,4096]{3,2,1,0:T(8,128)(2,1)}, u32[]{:S(2)}, u32[]{:S(2)}) %all-to-all-start.1) | async-done | bytes 1048608 | tf_op jit(solution)/shard_map/all_to_all | solution.py:128
  359.8 3.4 scatter_fusion
  (66 shorter events, 10.1 us)
Async XLA Ops:
  7.2 287.9 %copy-start = (bf16[2048,768]{1,0:T(8,128)(2,1)S(1)}, bf16[2048,768]{1,0:T(8,128)(2,1)}, u32[]{:S(2)}) copy-start(bf16[2048,768]{1,0:T(8,128)(2,1)} %param.27) | copy-start | bytes 9437188
  7.2 8.8 %copy-start.8 = (f32[4,128]{1,0:T(4,128)S(1)}, f32[4,128]{1,0:T(4,128)}, u32[]{:S(2)}) copy-start(f32[4,128]{1,0:T(4,128)} %param.20) | copy-start | bytes 6148
  7.2 10.8 %copy-start.1 = (s32[1,2048]{1,0:T(1,128)S(1)}, s32[1,2048]{1,0:T(1,128)}, u32[]{:S(2)}) copy-start(s32[1,2048]{1,0:T(1,128)} %param.19) | copy-start | bytes 24580
  7.2 130.3 %all-gather.4.cloned.1.call-start = ((), (), s32[]{:S(2)}) async-start(), calls=%async_computation.3 | async-start | bytes 17825792 | tf_op jit(solution)/shard_map/all_gather | solution.py:57
  13.7 186.4 %all-gather.6.cloned.1.call-start = ((), (), s32[]{:S(2)}) async-start(), calls=%async_computation.4 | async-start | bytes 4718592 | tf_op jit(solution)/shard_map/all_gather | solution.py:99
  137.5 5.1 %copy-start.5 = (bf16[128,8,2,128]{3,2,1,0:T(2,128)(2,1)S(1)}, bf16[128,8,2,128]{3,2,1,0:T(2,128)(2,1)}, u32[]{:S(2)}) copy-start(bf16[128,8,2,128]{3,2,1,0:T(2,128)(2,1)} %reshape.141) | copy-start | bytes 1572868
  145.1 3.6 copy-start.2
  166.0 37.4 %copy-start.11 = (f32[2048]{0:T(1024)S(1)}, f32[2048]{0:T(1024)}, u32[]{:S(2)}) copy-start(f32[2048]{0:T(1024)} %param.22) | copy-start | bytes 24580
  166.0 94.6 %reduce-scatter.2.cloned.1.call-start = ((), (), s32[]{:S(2)}) async-start(), calls=%async_computation.5 | async-start | bytes 4718592 | tf_op jit(solution)/shard_map/reduce_scatter | solution.py:104
  200.1 3.4 copy-start.4
  222.7 40.2 %copy-start.7 = (f32[2048]{0:T(1024)S(1)}, f32[2048]{0:T(1024)}, u32[]{:S(2)}) copy-start(f32[2048]{0:T(1024)} %param.26) | copy-start | bytes 24580
  222.7 72.4 %all-gather.8.cloned.1.call-start = ((), (), s32[]{:S(2)}) async-start(), calls=%async_computation.6 | async-start | bytes 4718592 | tf_op jit(solution)/shard_map/all_gather | solution.py:113
  262.1 0.8 copy-start.6
  263.9 42.8 %copy-start.9 = (s32[1,256]{1,0:T(1,128)S(1)}, s32[1,256]{1,0:T(1,128)}, u32[]{:S(2)}) copy-start(s32[1,256]{1,0:T(1,128)} %param.28) | copy-start | bytes 3076
  263.9 43.6 %copy-start.10 = (s32[1,256]{1,0:T(1,128)S(1)}, s32[1,256]{1,0:T(1,128)}, u32[]{:S(2)}) copy-start(s32[1,256]{1,0:T(1,128)} %param.29) | copy-start | bytes 3076
  301.8 25.9 %all-to-all-start = ((bf16[8,128,768]{2,1,0:T(8,128)(2,1)}), bf16[8,128,768]{2,1,0:T(8,128)(2,1)}, u32[]{:S(2)}, u32[]{:S(2)}) async-start(bf16[8,128,768]{2,1,0:T(8,128)(2,1)} %bitcast.71), calls=%async_computation.1 | async-start | bytes 3145728 | tf_op jit(solution)/shard_map/all_to_all | solution.py:117
  329.3 1.2 copy-start.3
  334.3 24.4 %all-to-all-start.1 = ((bf16[16,1,8,4096]{3,2,1,0:T(8,128)(2,1)}), bf16[16,1,8,4096]{3,2,1,0:T(8,128)(2,1)}, u32[]{:S(2)}, u32[]{:S(2)}) async-start(bf16[16,1,8,4096]{3,2,1,0:T(8,128)(2,1)} %bitcast.69), calls=%async_computation.2 | async-start | bytes 2097152 | tf_op jit(solution)/shard_map/all_to_all | solution.py:128
Sparse Core Ops, SparseCore 0:
  13.9 123.6 all-gather.3
  166.1 33.9 all-gather.5
  222.8 37.7 reduce-scatter.1
  264.0 31.0 all-gather.7
where the time goes:
time: 370 us
  waiting for transfers between devices  247 us (67%)
  matrix products  42.3 us (11%)
  local copies, waits for them, and re-layouts  36.7 us (10%)
  other arithmetic  16.7 us (5%)
  between operations  15.3 us (4%)
  starting transfers between devices  11.6 us (3%)
    all_gather x1, waiting for transfers between devices, body(): all_kv = lax.all_gather(own_kv, 'tok', axis=0, tiled=True)  112 us
    reduce_scatter x1, waiting for transfers between devices, body(): lax.psum_scatter(jnp.dot(hidden, down_weight, preferred_element_type=jnp....  37.9 us
    all_gather x1, waiting for transfers between devices, body(): gathered = lax.all_gather(residual_mid, 'req', axis=0, tiled=True)  33.9 us
    all_gather x1, waiting for transfers between devices, body(): lax.all_gather(next_normed, 'req', axis=0, tiled=True)  31.2 us
    all_to_all x1, waiting for transfers between devices, body(): lax.all_to_all(projected_cols, 'req', split_axis=0, concat_axis=1, tiled=...  18.2 us
    all_to_all x1, waiting for transfers between devices, body(): lax.all_to_all(outgoing, 'tok', split_axis=0, concat_axis=0, tiled=True)  14.1 us
    dot_general x1, matrix products, body(): jnp.dot(hidden, down_weight, preferred_element_type=jnp.float32)  12.4 us
    dot_general x1, matrix products, body(): jnp.einsum('hmqk,khe->hmqe', weights.astype(jnp.bfloat16), value_split, p...  8.27 us
  transfers between devices with their start and end apart: 6, of which 6 were waited for; matrix products, arithmetic and copies ran while one was open for 5% of the time, Pallas kernels for 0%

commit v1 on v0

--- a/solution.py
+++ b/solution.py
@@ -96,7 +96,9 @@
         layer_input.astype(jnp.float32)
         + jnp.dot(attention, out_weight, preferred_element_type=jnp.float32)
     ).astype(jnp.bfloat16)
-    gathered = lax.all_gather(residual_mid, "req", axis=0, tiled=True)
+    gathered = jnp.concatenate(
+        lax.all_to_all(jnp.stack([residual_mid] * lax.axis_size("req")), "req", 0, 0), axis=0
+    )
     normed = (rms_rows(gathered.astype(jnp.float32)) * ffn_gain).astype(jnp.bfloat16)
     gate_proj = jnp.dot(normed, gate_weight, preferred_element_type=jnp.float32)
     up_proj = jnp.dot(normed, up_weight, preferred_element_type=jnp.float32)

time: 370 us -> 389 us (1.051)
  blocking collectives: 0 us -> 54.4 us
  waiting for transfers between devices: 247 us -> 213 us
    all_to_all x0 -> x1, blocking collectives: none -> 54.4 us  [body(): lax.all_to_all(jnp.stack([residual_mid] * lax.axis_size('req')), 'req', 0...]
    all_gather x1 -> x0, waiting for transfers between devices: 33.9 us -> none  [body(): gathered = lax.all_gather(residual_mid, 'req', axis=0, tiled=True)]
    unnamed x28 -> x32, local copies, waits for them, and re-layouts: 8.25 us -> 10 us
  transfers between devices with their start and end apart: 6 -> 5, of which waited for: 6 -> 5; matrix products, arithmetic and copies ran while one was open for 5% -> 4% of each run, Pallas kernels for 0% -> 0%
where the time goes in v1:
time: 389 us; the launch traced here: 388 us
  waiting for transfers between devices  213 us (55%)
  blocking collectives  54.4 us (14%)
  matrix products  39.1 us (10%)
  local copies, waits for them, and re-layouts  39 us (10%)
  other arithmetic  15.3 us (4%)
  between operations  15.3 us (4%)
  starting transfers between devices  11.4 us (3%)
    all_gather x1, waiting for transfers between devices, body(): all_kv = lax.all_gather(own_kv, 'tok', axis=0, tiled=True)  112 us
    all_to_all x1, blocking collectives, body(): lax.all_to_all(jnp.stack([residual_mid] * lax.axis_size('req')), 'req', 0...  54.4 us
    reduce_scatter x1, waiting for transfers between devices, body(): lax.psum_scatter(jnp.dot(hidden, down_weight, preferred_element_type=jnp....  38 us
    all_gather x1, waiting for transfers between devices, body(): lax.all_gather(next_normed, 'req', axis=0, tiled=True)  31 us
    all_to_all x1, waiting for transfers between devices, body(): lax.all_to_all(projected_cols, 'req', split_axis=0, concat_axis=1, tiled=...  18.2 us
    all_to_all x1, waiting for transfers between devices, body(): lax.all_to_all(outgoing, 'tok', split_axis=0, concat_axis=0, tiled=True)  14.1 us
    dot_general x1, matrix products, body(): jnp.dot(hidden, down_weight, preferred_element_type=jnp.float32)  12 us
    unnamed x32, local copies, waits for them, and re-layouts  10 us
  transfers between devices with their start and end apart: 5, of which 5 were waited for; matrix products, arithmetic and copies ran while one was open for 4% of the time, Pallas kernels for 0%

profile of v1, /device:TPU:0, one launch (start us, length us, event | category | flops | bytes accessed | tf_op | source)
XLA Modules:
  0.0 387.9 jit_solution(7122246752290326810)
XLA Ops:
  7.2 2.2 copy.47
  9.4 2.0 copy.48
  11.5 2.2 pad_maximum_fusion
  13.8 2.2 reshape.155
  18.0 6.5 %gather_fusion = s32[1152]{0:T(1024)S(1)} fusion(s32[2048]{0:T(1024)S(1)} %bitcast.74, s32[2048]{0:T(1024)S(1)} %pad_clamp_fusion), kind=kCustom, calls=%fused_computation | custom fusion | bytes 13824 | tf_op jit(solution)/shard_map/jit(_take)/gather | solution.py:68
  25.6 112.0 %all-gather.3.cloned.1.call-done = bf16[2048,4096]{0,1:T(8,128)(2,1)} async-done(((bf16[128,4096]{0,1:T(8,128)(2,1)}), bf16[2048,4096]{0,1:T(8,128)(2,1)}) %all-gather.3.cloned.1.call-update) | async-done | bytes 16777232 | tf_op jit(solution)/shard_map/all_gather | solution.py:57
  137.5 5.1 %pad_dynamic-slice_fusion.1 = (bf16[1152,2048]{0,1:T(8,128)(2,1)}, bf16[1152,2048]{0,1:T(8,128)(2,1)S(1)}) fusion(s32[]{:T(128)S(6)} %select_n.70, s32[]{:T(128)S(6)} %add.179, bf16[2048,4096]{0,1:T(8,128)(2,1)} %all-gather.3.cloned.1.call-done), kind=kLoop, calls=%fused_computation.5 | loop fusion | bytes 26214408 | tf_op jit(solution)/shard_map/slice | solution.py:64
  142.6 2.5 fusion.2
  145.1 2.3 fusion.3
  147.4 1.3 copy-done.2
  148.7 8.3 %broadcast_divide_fusion = f32[8,2,128,256]{3,2,1,0:T(8,128)S(1)} fusion(f32[8,2,128]{2,1,0:T(2,128)S(1)} %fusion.3, bf16[1152,8,256,1]{0,2,3,1:T(8,128)(2,1)} %bitcast.78, f32[8,2,1152,128]{3,2,1,0:T(8,128)} %copy-done.2, f32[8,2,128]{2,1,0:T(2,128)S(1)} %broadcast_maximum_fusion, pred[128,1152]{0,1:T(8,128)(4,1)S(1)} %compare_and_fusion), kind=kOutput, calls=%fused_computation.39 | convolution fusion | flops 1220280320 | bytes 16416768 | tf_op jit(solution)/shard_map/hmqk,khe->hmqe/dot_general | solution.py:82
  157.2 1.1 fusion.20
  158.3 2.0 copy.53
  160.3 4.9 %fusion.12 = bf16[128,2048]{1,0:T(8,128)(2,1)S(1)} fusion(bf16[128,2048]{0,1:T(8,128)(2,1)} %bitcast.80, bf16[2048,2048]{1,0:T(8,128)(2,1)} %param.21, bf16[128,2048]{1,0:T(8,128)(2,1)} %param.15), kind=kOutput, calls=%fused_computation.24 | convolution fusion | flops 1074528256 | bytes 9961472 | tf_op jit(solution)/shard_map/dot_general | solution.py:97
  165.7 54.4 %all_to_all.29 = bf16[8,128,2048]{2,1,0:T(8,128)(2,1)S(1)} all-to-all(bf16[8,128,2048]{2,1,0:T(8,128)(2,1)S(1)} %stack.2), channel_id=1, replica_groups=mesh['req'=8,'tok'=16] {'req'}, dimensions={0} | all-to-all | bytes 8388608 | tf_op jit(solution)/shard_map/all_to_all | solution.py:100
  222.1 2.0 copy-done.5
  224.1 4.8 %fusion.35 = f32[1024,704]{0,1:T(8,128)} fusion(bf16[1024,2048]{1,0:T(8,128)(2,1)S(1)} %fusion.1, bf16[2048,704]{0,1:T(8,128)(2,1)S(1)} %copy-done.13), kind=kOutput, calls=%fused_computation.79 | convolution fusion | flops 2952790016 | bytes 9961472 | tf_op jit(solution)/shard_map/dot_general | solution.py:103
  228.9 12.0 %convolution_convert_fusion = bf16[1024,2048]{1,0:T(8,128)(2,1)} fusion(bf16[704,2048]{1,0:T(8,128)(2,1)} %param.25, f32[1024,704]{0,1:T(8,128)} %fusion.35, bf16[1024,2048]{1,0:T(8,128)(2,1)} %copy-done.5, bf16[2048,704]{0,1:T(8,128)(2,1)} %param.24), kind=kOutput, calls=%fused_computation.21 | convolution fusion | flops 5912002560 | bytes 17039360 | tf_op jit(solution)/shard_map/dot_general | solution.py:107
  241.0 38.0 %reduce-scatter.2.cloned.1.call-done = bf16[128,2048]{1,0:T(8,128)(2,1)} async-done(((bf16[1024,2048]{1,0:T(8,128)(2,1)}), bf16[128,2048]{1,0:T(8,128)(2,1)}) %reduce-scatter.2.cloned.1.call-update) | async-done | bytes 524304 | tf_op jit(solution)/shard_map/reduce_scatter | solution.py:106
  279.0 1.5 fusion.13
  282.2 31.0 %all-gather.5.cloned.1.call-done = bf16[1024,2048]{1,0:T(8,128)(2,1)} async-done(((bf16[128,2048]{1,0:T(8,128)(2,1)}), bf16[1024,2048]{1,0:T(8,128)(2,1)}) %all-gather.5.cloned.1.call-update) | async-done | bytes 4194320 | tf_op jit(solution)/shard_map/all_gather | solution.py:115
  313.3 6.8 %convolution_convert_fusion.1 = bf16[1024,768]{1,0:T(8,128)(2,1)} fusion(bf16[1024,2048]{1,0:T(8,128)(2,1)} %all-gather.5.cloned.1.call-done, bf16[2048,768]{1,0:T(8,128)(2,1)S(1)} %copy-done), kind=kOutput, calls=%fused_computation.25 | convolution fusion | flops 3222011904 | bytes 8912896 | tf_op jit(solution)/shard_map/dot_general | solution.py:114
  320.0 4.3 %all-to-all-start.1 = ((bf16[8,128,768]{2,1,0:T(8,128)(2,1)}), bf16[8,128,768]{2,1,0:T(8,128)(2,1)}, u32[]{:S(2)}, u32[]{:S(2)}) async-start(bf16[8,128,768]{2,1,0:T(8,128)(2,1)} %bitcast.81), calls=%async_computation.2 | async-start | bytes 3145728 | tf_op jit(solution)/shard_map/all_to_all | solution.py:119
  326.4 1.2 sort.35
  327.7 18.2 %all-to-all-done.1 = bf16[8,128,768]{2,1,0:T(8,128)(2,1)} async-done(((bf16[8,128,768]{2,1,0:T(8,128)(2,1)}), bf16[8,128,768]{2,1,0:T(8,128)(2,1)}, u32[]{:S(2)}, u32[]{:S(2)}) %all-to-all-start.1) | async-done | bytes 1572896 | tf_op jit(solution)/shard_map/all_to_all | solution.py:119
  345.9 1.6 copy.61
  347.5 1.1 copy-done.3
  349.7 2.8 gather_fusion.1
  352.5 7.0 %all-to-all-start.2 = ((bf16[16,1,8,4096]{3,2,1,0:T(8,128)(2,1)}), bf16[16,1,8,4096]{3,2,1,0:T(8,128)(2,1)}, u32[]{:S(2)}, u32[]{:S(2)}) async-start(bf16[16,1,8,4096]{3,2,1,0:T(8,128)(2,1)} %bitcast.79), calls=%async_computation.3 | async-start | bytes 2097152 | tf_op jit(solution)/shard_map/all_to_all | solution.py:130
  361.0 1.9 slice.52
  362.9 14.1 %all-to-all-done.2 = bf16[16,1,8,4096]{3,2,1,0:T(8,128)(2,1)} async-done(((bf16[16,1,8,4096]{3,2,1,0:T(8,128)(2,1)}), bf16[16,1,8,4096]{3,2,1,0:T(8,128)(2,1)}, u32[]{:S(2)}, u32[]{:S(2)}) %all-to-all-start.2) | async-done | bytes 1048608 | tf_op jit(solution)/shard_map/all_to_all | solution.py:130
  378.0 3.4 scatter_fusion
  (70 shorter events, 12.1 us)
Async XLA Ops:
  7.2 306.1 %copy-start = (bf16[2048,768]{1,0:T(8,128)(2,1)S(1)}, bf16[2048,768]{1,0:T(8,128)(2,1)}, u32[]{:S(2)}) copy-start(bf16[2048,768]{1,0:T(8,128)(2,1)} %param.27) | copy-start | bytes 9437188
  7.2 8.8 %copy-start.10 = (f32[4,128]{1,0:T(4,128)S(1)}, f32[4,128]{1,0:T(4,128)}, u32[]{:S(2)}) copy-start(f32[4,128]{1,0:T(4,128)} %param.20) | copy-start | bytes 6148
  7.2 10.8 %copy-start.1 = (s32[1,2048]{1,0:T(1,128)S(1)}, s32[1,2048]{1,0:T(1,128)}, u32[]{:S(2)}) copy-start(s32[1,2048]{1,0:T(1,128)} %param.19) | copy-start | bytes 24580
  7.2 130.3 %all-gather.3.cloned.1.call-start = ((), (), s32[]{:S(2)}) async-start(), calls=%async_computation.4 | async-start | bytes 17825792 | tf_op jit(solution)/shard_map/all_gather | solution.py:57
  13.7 265.2 %reduce-scatter.2.cloned.1.call-start = ((), (), s32[]{:S(2)}) async-start(), calls=%async_computation.5 | async-start | bytes 4718592 | tf_op jit(solution)/shard_map/reduce_scatter | solution.py:106
  137.5 5.1 %copy-start.6 = (bf16[128,8,2,128]{3,2,1,0:T(2,128)(2,1)S(1)}, bf16[128,8,2,128]{3,2,1,0:T(2,128)(2,1)}, u32[]{:S(2)}) copy-start(bf16[128,8,2,128]{3,2,1,0:T(2,128)(2,1)} %reshape.155) | copy-start | bytes 1572868
  145.1 3.6 copy-start.2
  165.2 55.0 %copy-start.4 = (bf16[128,2048]{1,0:T(8,128)(2,1)}, bf16[128,2048]{1,0:T(8,128)(2,1)S(1)}, u32[]{:S(2)}) copy-start(bf16[128,2048]{1,0:T(8,128)(2,1)S(1)} %fusion.12) | copy-start | bytes 1572868
  220.2 0.9 copy-start.8
  221.1 3.0 copy-start.13
  222.1 2.0 copy-start.5
  240.9 40.3 %copy-start.9 = (f32[2048]{0:T(1024)S(1)}, f32[2048]{0:T(1024)}, u32[]{:S(2)}) copy-start(f32[2048]{0:T(1024)} %param.26) | copy-start | bytes 24580
  240.9 72.3 %all-gather.5.cloned.1.call-start = ((), (), s32[]{:S(2)}) async-start(), calls=%async_computation.6 | async-start | bytes 4718592 | tf_op jit(solution)/shard_map/all_gather | solution.py:115
  280.4 0.8 copy-start.7
  282.2 42.6 %copy-start.11 = (s32[1,256]{1,0:T(1,128)S(1)}, s32[1,256]{1,0:T(1,128)}, u32[]{:S(2)}) copy-start(s32[1,256]{1,0:T(1,128)} %param.28) | copy-start | bytes 3076
  282.2 43.4 %copy-start.12 = (s32[1,256]{1,0:T(1,128)S(1)}, s32[1,256]{1,0:T(1,128)}, u32[]{:S(2)}) copy-start(s32[1,256]{1,0:T(1,128)} %param.29) | copy-start | bytes 3076
  320.0 25.9 %all-to-all-start.1 = ((bf16[8,128,768]{2,1,0:T(8,128)(2,1)}), bf16[8,128,768]{2,1,0:T(8,128)(2,1)}, u32[]{:S(2)}, u32[]{:S(2)}) async-start(bf16[8,128,768]{2,1,0:T(8,128)(2,1)} %bitcast.81), calls=%async_computation.2 | async-start | bytes 3145728 | tf_op jit(solution)/shard_map/all_to_all | solution.py:119
  347.5 1.2 copy-start.3
  352.5 24.5 %all-to-all-start.2 = ((bf16[16,1,8,4096]{3,2,1,0:T(8,128)(2,1)}), bf16[16,1,8,4096]{3,2,1,0:T(8,128)(2,1)}, u32[]{:S(2)}, u32[]{:S(2)}) async-start(bf16[16,1,8,4096]{3,2,1,0:T(8,128)(2,1)} %bitcast.79), calls=%async_computation.3 | async-start | bytes 2097152 | tf_op jit(solution)/shard_map/all_to_all | solution.py:130
Sparse Core Ops, SparseCore 0:
  13.9 123.6 all-gather.2
  241.0 37.8 reduce-scatter.1
  282.3 30.8 all-gather.4
